TPU v7x, 32 devices: a whole 2x2x4 slice. The times are simulated.
32 devices in a mesh: layer: 8 (over y, x, core), dp: 4 (over z).
Axes of the slice: x: 2, y: 2, z: 4, core: 2. Of those that a mesh axis runs over, the one named last changes fastest.
Arguments:
- images: float32 [8, 16, 16, 128], P('dp'), may hold values from -6 to 6
- weights: bfloat16 [32, 3, 3, 128, 128], P('layer'), may hold values from -0.1875 to 0.1875
- biases: float32 [32, 128], P('layer'), may hold values from -3 to 3
- end_grad: float32 [8, 16, 16, 128], P('dp'), may hold values from -6 to 6
Outputs:
- interval_ends: float32 [8, 8, 16, 16, 128], P('layer', 'dp')
- start_adjoint: float32 [8, 8, 16, 16, 128], P('layer', 'dp')
- weight_grad: float32 [32, 3, 3, 128, 128], P('layer')
- bias_grad: float32 [32, 128], P('layer')
All inputs are finite; a program needn't handle non-finite values.
Results may differ from a plain program's by a relative error of at most 0.012.
The roundings to bfloat16 on the way count: a program that leaves them out, or rounds other values in their place, can miss the bound.
Values sent between devices are 32-bit elements; how exact they have to be, the bound alone decides.
A program may use at most 128 MiB of HBM per device.

v0:
```python
import functools

import jax
import jax.numpy as jnp
from jax import lax
from jax.experimental import pallas as pl
from jax.experimental.pallas import tpu as pltpu
from jax.sharding import PartitionSpec as P

step_size = 0.25
MESH = pl.DeviceIdType.MESH
low = jnp.bfloat16


def dot(a, b, contract=((1,), (0,))):
    return lax.dot_general(a, b, (contract, ((), ())), preferred_element_type=jnp.float32)


NT = ((1,), (1,))
TN = ((0,), (0,))


def kernel(
    dims,
    images_in,
    weights_in,
    biases_in,
    end_grad_in,
    ends_out,
    start_out,
    wg_out,
    bg_out,
    images,
    weights,
    biases,
    end_grad,
    load_sems,
    flipped,
    window,
    maps,
    states_low,
    slopes,
    states_all,
    adj_all,
    residue,
    gathered,
    spread,
    error,
    map_send,
    map_recv,
    hand_send,
    out_send,
    out_recv,
    back_send,
    back_recv,
    right_send,
    left_send,
    line_recv,
):
    groups, parts, count, height, width, images_all = dims
    rows, channels = images_in.shape
    blocks = weights_in.shape[0]
    share = rows // groups
    me = lax.axis_index("layer")
    z = lax.axis_index("dp")
    not_first = z > 0
    not_last = z < parts - 1

    def others(body):
        def step(ahead, _):
            body(ahead, lax.rem(me + ahead, groups))
            return 0

        lax.fori_loop(1, groups, step, 0)

    loads = [
        pltpu.make_async_copy(source, target, load_sems.at[i])
        for i, (source, target) in enumerate(
            ((weights_in, weights), (images_in, images), (biases_in, biases), (end_grad_in, end_grad))
        )
    ]
    for load in loads:
        load.start()
    barrier = pltpu.get_barrier_semaphore()
    others(lambda ahead, to: pl.semaphore_signal(barrier, inc=1, device_id={"layer": to}, device_id_type=MESH))

    @pl.when(not_first)
    def _():
        pl.semaphore_signal(barrier, inc=1, device_id={"dp": z - 1}, device_id_type=MESH)

    @pl.when(not_last)
    def _():
        pl.semaphore_signal(barrier, inc=1, device_id={"dp": z + 1}, device_id_type=MESH)

    for load in loads:
        load.wait()
    centre = slice(4 * channels, 5 * channels)
    total = weights[0, centre, :].astype(jnp.float32)
    for n in range(1, blocks):
        total = total + weights[n, centre, :].astype(jnp.float32)
    maps[me] = step_size * total

    neighbours = jnp.where(not_first, 1, 0) + jnp.where(not_last, 1, 0)
    pl.semaphore_wait(barrier, groups - 1 + neighbours)

    def map_copy(slot, to):
        return pltpu.make_async_remote_copy(
            src_ref=maps.at[slot],
            dst_ref=maps.at[slot],
            send_sem=map_send.at[to],
            recv_sem=map_recv.at[slot],
            device_id={"layer": to},
            device_id_type=MESH,
        )

    last = groups - 1
    after = lax.rem(me + 1, groups)
    before = lax.rem(me + last, groups)
    pair = 2 if groups % 2 == 0 else 1
    partner = me + 1 - 2 * lax.rem(me, 2) if pair == 2 else me

    def same_side(body):
        def step(ahead, _):
            body(lax.rem(me + pair * ahead, groups))
            return 0

        lax.fori_loop(1, groups // pair, step, 0)

    map_copy(me, after).start()
    if pair == 2:

        @pl.when(partner != after)
        def _():
            map_copy(me, partner).start()

    def send_map(to):
        if pair == 1:

            @pl.when(to != after)
            def _():
                map_copy(me, to).start()

        else:
            map_copy(me, to).start()

    same_side(send_map)

    def hand_copy(slot):
        return pltpu.make_async_remote_copy(
            src_ref=maps.at[slot],
            dst_ref=maps.at[slot],
            send_sem=hand_send.at[slot],
            recv_sem=map_recv.at[slot],
            device_id={"layer": partner},
            device_id_type=MESH,
        )

    def is_handed(slot):
        return lax.rem(slot + 1, groups) != partner

    def hand_on(slot):
        @pl.when((slot != before) | (me == 0))
        def _():
            map_copy(slot, me).wait_recv()

        if pair == 2:

            @pl.when(is_handed(slot))
            def _():
                hand_copy(slot).start()

    zero_row = jnp.zeros((count, 1, width, 3 * channels), low)
    window[:, 0:1] = zero_row
    window[:, height + 1 : height + 2] = zero_row

    def prepare(n, _):
        for tap in range(9):
            flipped[n, :, tap * channels : (tap + 1) * channels] = weights[
                n, (8 - tap) * channels : (9 - tap) * channels, :
            ]
        wg_out[n] = jnp.zeros(wg_out.shape[1:], jnp.float32)
        return 0

    lax.fori_loop(0, blocks, prepare, 0)
    bg_out[...] = jnp.zeros(bg_out.shape, jnp.float32)

    column = lax.rem(lax.broadcasted_iota(jnp.int32, (rows, channels), 0), width)

    def patches(field):
        left = jnp.where(column == 0, 0.0, pltpu.roll(field, 1, 0))
        right = jnp.where(column == width - 1, 0.0, pltpu.roll(field, rows - 1, 0))
        shape = (count, height, width, channels)
        window[:, 1 : height + 1, :, 0:channels] = left.astype(low).reshape(shape)
        window[:, 1 : height + 1, :, channels : 2 * channels] = field.astype(low).reshape(shape)
        window[:, 1 : height + 1, :, 2 * channels : 3 * channels] = right.astype(low).reshape(shape)
        return jnp.concatenate(
            [window[:, i : i + height].reshape(rows, 3 * channels) for i in range(3)], axis=1
        )

    def apply_map(field, slot):
        return field + dot(field.astype(low), maps[slot].astype(low))

    def apply_flipped(field, slot):
        return field + dot(field.astype(low), maps[slot].astype(low), NT)

    def advance(n, state):
        return state + step_size * jnp.tanh(dot(patches(state), weights[n]) + biases[pl.ds(n, 1), :])

    def trajectory(part, state):
        def step(n, state):
            states_low[n, part] = state.astype(low)
            activation = jnp.tanh(dot(patches(state), weights[n]) + biases[pl.ds(n, 1), :])
            slopes[n, part] = activation
            return state + step_size * activation

        return lax.fori_loop(0, blocks, step, state)

    def change_of(n, part, adjoint):
        slope = slopes[n, part]
        return step_size * (1.0 - slope * slope) * adjoint

    def retreat(part, adjoint):
        def step(i, adjoint):
            n = blocks - 1 - i
            return adjoint + dot(patches(change_of(n, part, adjoint)), flipped[n], NT)

        return lax.fori_loop(0, blocks, step, adjoint)

    divisor = 1.0 / images_all

    def sweep(part, adjoint):
        def step(i, adjoint):
            n = blocks - 1 - i
            change = change_of(n, part, adjoint)
            bg_out[pl.ds(n, 1), :] += jnp.sum(change, axis=0, keepdims=True) * divisor
            spots = patches(change)
            adjoint = adjoint + dot(spots, flipped[n], NT)
            grads = dot(states_low[n, part], spots, TN) * divisor
            for tap in range(9):
                wg_out[n, (8 - tap) * channels : (9 - tap) * channels, :] += grads[
                    :, tap * channels : (tap + 1) * channels
                ]
            return adjoint

        return lax.fori_loop(0, blocks, step, adjoint)

    def rows_of(slot):
        return pl.ds(pl.multiple_of(slot * share, share), share)

    def out_copy(phase, source, to):
        return pltpu.make_async_remote_copy(
            src_ref=residue.at[phase, rows_of(to)],
            dst_ref=gathered.at[phase, source],
            send_sem=out_send.at[phase, to],
            recv_sem=out_recv.at[phase, source],
            device_id={"layer": to},
            device_id_type=MESH,
        )

    def back_copy(phase, source, to):
        return pltpu.make_async_remote_copy(
            src_ref=spread.at[phase, to],
            dst_ref=error.at[phase, rows_of(source)],
            send_sem=back_send.at[phase, to],
            recv_sem=back_recv.at[phase, source],
            device_id={"layer": to},
            device_id_type=MESH,
        )

    def chain_start(phase, value):
        residue[phase] = value
        others(lambda ahead, to: out_copy(phase, me, to).start())
        gathered[phase, me] = residue[phase, rows_of(me)]

    def chain_scan(phase):
        def step(i, carried):
            k = i if phase == 0 else groups - 1 - i

            @pl.when(k != me)
            def _():
                spread[phase, k] = carried
                back_copy(phase, me, k).start()
                out_copy(phase, k, me).wait_recv()

            @pl.when(k == me)
            def _():
                error[phase, rows_of(me)] = carried

            mapped = apply_map(carried, k) if phase == 0 else apply_flipped(carried, k)
            return mapped + gathered[phase, k]

        lax.fori_loop(0, groups, step, jnp.zeros((share, channels), jnp.float32))

    def chain_finish(phase):
        others(lambda ahead, to: back_copy(phase, to, me).wait_recv())
        return error[phase]

    line = (states_all, adj_all)

    piece = rows // count

    def line_copy(which, block, part, to, sends):
        where = line[which].at[block, part * piece : (part + 1) * piece]
        return pltpu.make_async_remote_copy(
            src_ref=where,
            dst_ref=where,
            send_sem=sends.at[which, block, part],
            recv_sem=line_recv.at[which, block, part],
            device_id={"dp": to},
            device_id_type=MESH,
        )

    def go_right(which, block, part):
        @pl.when(not_last)
        def _():
            line_copy(which, block, part, z + 1, right_send).start()

    def go_left(which, block, part):
        @pl.when(not_first)
        def _():
            line_copy(which, block, part, z - 1, left_send).start()

    def line_start(which):
        for part in range(count):
            go_right(which, z, part)
            go_left(which, z, part)

    def line_round(which, away):
        for part in range(count):

            @pl.when(z - away >= 0)
            def _():
                line_copy(which, z - away, part, z, right_send).wait_recv()
                go_right(which, z - away, part)

            @pl.when(z + away < parts)
            def _():
                line_copy(which, z + away, part, z, left_send).wait_recv()
                go_left(which, z + away, part)

    def nth_other(i):
        back_side = parts - 1 - z
        paired = jnp.where(z < back_side, z, back_side)
        near = i // 2 + 1
        near_part = jnp.where(i % 2 == 0, z - near, z + near)
        far = i - paired + 1
        far_part = jnp.where(z > back_side, z - far, z + far)
        return jnp.where(i < 2 * paired, near_part, far_part)

    def other_trajectory(i):
        part = nth_other(i)
        trajectory(part, states_all[part])

    start_image = images[...]

    @pl.when(me != 0)
    def _():
        map_copy(before, me).wait_recv()

    starts = jnp.where(me == 0, start_image, apply_map(start_image, jnp.where(me == 0, me, before)))
    relaxed = lax.fori_loop(0, blocks, advance, starts)
    chain_start(0, relaxed - apply_map(start_image, me))

    same_side(hand_on)

    def wait_map(ahead, source):
        @pl.when((lax.rem(source - me + groups, pair) != 0) & ((source != before) | (me == 0)))
        def _():
            map_copy(source, me).wait_recv()

    if pair == 2:
        others(wait_map)
    end = end_grad[...]
    ends_adj = jnp.where(me == last, end, apply_flipped(end, after))
    back = apply_flipped(end, me)
    chain_scan(0)
    corrected = starts + chain_finish(0)
    states_all[z] = corrected
    line_start(0)
    ends_out[...] = trajectory(z, corrected)

    chain_start(1, retreat(z, ends_adj) - back)
    if parts > 1:
        line_round(0, 1)
        other_trajectory(0)
    chain_scan(1)
    if parts > 2:
        line_round(0, 2)
        other_trajectory(1)
    adjoint = ends_adj + chain_finish(1)
    adj_all[z] = adjoint
    line_start(1)
    start_out[...] = sweep(z, adjoint)
    for i in range(2, parts - 1):
        line_round(0, i + 1)
        other_trajectory(i)
    for i in range(parts - 1):
        line_round(1, i + 1)
        part = nth_other(i)
        sweep(part, adj_all[part])

    def map_sent(to):
        if pair == 1:

            @pl.when(to != after)
            def _():
                map_copy(me, to).wait_send()

        else:
            map_copy(me, to).wait_send()

            @pl.when(is_handed(to))
            def _():
                hand_copy(to).wait_send()

    map_copy(me, after).wait_send()
    if pair == 2:

        @pl.when(partner != after)
        def _():
            map_copy(me, partner).wait_send()

    same_side(map_sent)

    def sent(ahead, to):
        for phase in range(2):
            out_copy(phase, me, to).wait_send()
            back_copy(phase, me, to).wait_send()

    others(sent)
    for which in range(2):
        for away in range(parts):

            @pl.when((z - away >= 0) & not_last)
            def _():
                for part in range(count):
                    line_copy(which, z - away, part, z + 1, right_send).wait_send()

            @pl.when((z + away < parts) & not_first)
            def _():
                for part in range(count):
                    line_copy(which, z + away, part, z - 1, left_send).wait_send()


def shards(images, weights, biases, end_grad):
    groups = lax.axis_size("layer")
    parts = lax.axis_size("dp")
    count, height, width, channels = images.shape
    blocks = weights.shape[0]
    rows = count * height * width
    dims = (groups, parts, count, height, width, count * parts)
    f32 = jnp.float32
    share = rows // groups
    dma = pltpu.SemaphoreType.DMA
    vmem = pl.BlockSpec(memory_space=pltpu.VMEM)
    ends, start, wg, bg = pl.pallas_call(
        functools.partial(kernel, dims),
        out_shape=(
            pltpu.VMEM((rows, channels), f32),
            pltpu.VMEM((rows, channels), f32),
            pltpu.VMEM((blocks, 9 * channels, channels), f32),
            pltpu.VMEM((blocks, channels), f32),
        ),
        in_specs=[pl.BlockSpec(memory_space=pltpu.HBM)] * 4,
        out_specs=(vmem,) * 4,
        scratch_shapes=[
            pltpu.VMEM((rows, channels), f32),
            pltpu.VMEM((blocks, 9 * channels, channels), low),
            pltpu.VMEM((blocks, channels), f32),
            pltpu.VMEM((rows, channels), f32),
            dma((4,)),
            pltpu.VMEM((blocks, channels, 9 * channels), low),
            pltpu.VMEM((count, height + 2, width, 3 * channels), low),
            pltpu.VMEM((groups, channels, channels), f32),
            pltpu.VMEM((blocks, parts, rows, channels), low),
            pltpu.VMEM((blocks, parts, rows, channels), f32),
            pltpu.VMEM((parts, rows, channels), f32),
            pltpu.VMEM((parts, rows, channels), f32),
            pltpu.VMEM((2, rows, channels), f32),
            pltpu.VMEM((2, groups, share, channels), f32),
            pltpu.VMEM((2, groups, share, channels), f32),
            pltpu.VMEM((2, rows, channels), f32),
            dma((groups,)),
            dma((groups,)),
            dma((groups,)),
            dma((2, groups)),
            dma((2, groups)),
            dma((2, groups)),
            dma((2, groups)),
            dma((2, parts, count)),
            dma((2, parts, count)),
            dma((2, parts, count)),
        ],
        compiler_params=pltpu.CompilerParams(
            collective_id=0, has_side_effects=True, vmem_limit_bytes=61 << 20
        ),
    )(
        images.reshape(rows, channels),
        weights.reshape(blocks, 9 * channels, channels),
        biases,
        end_grad.reshape(rows, channels),
    )
    shape = (1,) + images.shape
    return (ends.reshape(shape), start.reshape(shape), wg.reshape(weights.shape), bg)


def solution(mesh):
    in_specs = (
        P("dp", None, None, None),
        P("layer", None, None, None, None),
        P("layer", None),
        P("dp", None, None, None),
    )
    out_specs = (
        P("layer", "dp", None, None, None),
        P("layer", "dp", None, None, None),
        P("layer", None, None, None, None),
        P("layer", None),
    )
    return jax.shard_map(shards, mesh=mesh, in_specs=in_specs, out_specs=out_specs, check_vma=False)
```

profile of v0, /device:TPU:0, one launch (start us, length us, event | category | flops | bytes accessed | tf_op | source)
XLA Modules:
  0.0 60.8 jit_solution(14629025748957901390)
XLA Ops:
  0.6 56.8 %shard_map.75 = (f32[512,128]{1,0:T(8,128)S(1)}, f32[512,128]{1,0:T(8,128)S(1)}, f32[4,1152,128]{2,1,0:T(8,128)S(1)}, f32[4,128]{1,0:T(4,128)S(1)}) custom-call(f32[512,128]{1,0:T(8,128)} %bitcast.10, bf16[4,1152,128]{2,1,0:T(8,128)(2,1)} %bitcast.9, f32[4,128]{1,0:T(4,128)} %biases_in.1, f32[512,128]{1,0:T(8,128)} %bitcast.11), custom_call_target="tpu_custom_call" | custom-call | tf_op jit(solution)/shard_map/pallas_call | solution.py:456
  57.4 0.7 %copy.12 = f32[1,2,16,16,128]{4,3,2,1,0:T(8,128)} copy(f32[1,2,16,16,128]{4,3,2,1,0:T(8,128)S(1)} %bitcast.8) | data formatting | bytes 524288
  58.1 0.7 %copy.13 = f32[1,2,16,16,128]{4,3,2,1,0:T(8,128)} copy(f32[1,2,16,16,128]{4,3,2,1,0:T(8,128)S(1)} %bitcast.7) | data formatting | bytes 524288
  58.8 0.6 copy.15
  59.4 1.4 %copy.14 = f32[4,3,3,128,128]{4,3,2,1,0:T(8,128)} copy(f32[4,3,3,128,128]{4,3,2,1,0:T(8,128)S(1)} %bitcast.6) | data formatting | bytes 4718592
where the time goes:
time: 60.9 us; the launch traced here: 60.8 us
  Pallas kernels  56.8 us (93%)
  local copies, waits for them, and re-layouts  3.39 us (6%)
  between operations  0.64 us (1%)
    pallas_call x1, Pallas kernels, shards(): pl.pallas_call(functools.partial(kernel, dims), out_shape=(pltpu.VMEM((ro...  56.8 us
    unnamed x4, local copies, waits for them, and re-layouts  3.39 us

commit v1 on v0

--- a/solution.py
+++ b/solution.py
@@ -187,14 +187,17 @@
     column = lax.rem(lax.broadcasted_iota(jnp.int32, (rows, channels), 0), width)
 
     def patches(field):
-        left = jnp.where(column == 0, 0.0, pltpu.roll(field, 1, 0))
-        right = jnp.where(column == width - 1, 0.0, pltpu.roll(field, rows - 1, 0))
-        shape = (count, height, width, channels)
-        window[:, 1 : height + 1, :, 0:channels] = left.astype(low).reshape(shape)
-        window[:, 1 : height + 1, :, channels : 2 * channels] = field.astype(low).reshape(shape)
-        window[:, 1 : height + 1, :, 2 * channels : 3 * channels] = right.astype(low).reshape(shape)
+        size = field.shape[0]
+        some = size // (height * width)
+        place = column[:size]
+        left = jnp.where(place == 0, 0.0, pltpu.roll(field, 1, 0))
+        right = jnp.where(place == width - 1, 0.0, pltpu.roll(field, size - 1, 0))
+        shape = (some, height, width, channels)
+        window[:some, 1 : height + 1, :, 0:channels] = left.astype(low).reshape(shape)
+        window[:some, 1 : height + 1, :, channels : 2 * channels] = field.astype(low).reshape(shape)
+        window[:some, 1 : height + 1, :, 2 * channels : 3 * channels] = right.astype(low).reshape(shape)
         return jnp.concatenate(
-            [window[:, i : i + height].reshape(rows, 3 * channels) for i in range(3)], axis=1
+            [window[:some, i : i + height].reshape(size, 3 * channels) for i in range(3)], axis=1
         )
 
     def apply_map(field, slot):
@@ -215,8 +218,8 @@
 
         return lax.fori_loop(0, blocks, step, state)
 
-    def change_of(n, part, adjoint):
-        slope = slopes[n, part]
+    def change_of(n, part, adjoint, at=0):
+        slope = slopes[n, part, at : at + adjoint.shape[0]]
         return step_size * (1.0 - slope * slope) * adjoint
 
     def retreat(part, adjoint):
@@ -228,14 +231,14 @@
 
     divisor = 1.0 / images_all
 
-    def sweep(part, adjoint):
+    def sweep(part, adjoint, at=0):
         def step(i, adjoint):
             n = blocks - 1 - i
-            change = change_of(n, part, adjoint)
+            change = change_of(n, part, adjoint, at)
             bg_out[pl.ds(n, 1), :] += jnp.sum(change, axis=0, keepdims=True) * divisor
             spots = patches(change)
             adjoint = adjoint + dot(spots, flipped[n], NT)
-            grads = dot(states_low[n, part], spots, TN) * divisor
+            grads = dot(states_low[n, part, at : at + adjoint.shape[0]], spots, TN) * divisor
             for tap in range(9):
                 wg_out[n, (8 - tap) * channels : (9 - tap) * channels, :] += grads[
                     :, tap * channels : (tap + 1) * channels
@@ -325,8 +328,8 @@
             go_right(which, z, part)
             go_left(which, z, part)
 
-    def line_round(which, away):
-        for part in range(count):
+    def line_round(which, away, pieces=range(count)):
+        for part in pieces:
 
             @pl.when(z - away >= 0)
             def _():
@@ -394,10 +397,15 @@
     for i in range(2, parts - 1):
         line_round(0, i + 1)
         other_trajectory(i)
-    for i in range(parts - 1):
+    for i in range(parts - 2):
         line_round(1, i + 1)
         part = nth_other(i)
         sweep(part, adj_all[part])
+    if parts > 1:
+        part = nth_other(parts - 2)
+        for i in range(count):
+            line_round(1, parts - 1, (i,))
+            sweep(part, adj_all[part, i * piece : (i + 1) * piece], i * piece)
 
     def map_sent(to):
         if pair == 1:

time: 60.9 us -> 60 us (0.985)
  Pallas kernels: 56.8 us -> 55.9 us
    pallas_call x1, Pallas kernels: 56.8 us -> 55.9 us  [shards(): pl.pallas_call(functools.partial(kernel, dims), out_shape=(pltpu.VMEM((ro...]
where the time goes in v1:
time: 60 us; the launch traced here: 59.9 us
  Pallas kernels  55.9 us (93%)
  local copies, waits for them, and re-layouts  3.39 us (6%)
  between operations  0.64 us (1%)
    pallas_call x1, Pallas kernels, shards(): pl.pallas_call(functools.partial(kernel, dims), out_shape=(pltpu.VMEM((ro...  55.9 us
    unnamed x4, local copies, waits for them, and re-layouts  3.39 us

profile of v1, /device:TPU:0, one launch (start us, length us, event | category | flops | bytes accessed | tf_op | source)
XLA Modules:
  0.0 59.9 jit_solution(12888683815408118689)
XLA Ops:
  0.6 55.9 %shard_map.75 = (f32[512,128]{1,0:T(8,128)S(1)}, f32[512,128]{1,0:T(8,128)S(1)}, f32[4,1152,128]{2,1,0:T(8,128)S(1)}, f32[4,128]{1,0:T(4,128)S(1)}) custom-call(f32[512,128]{1,0:T(8,128)} %bitcast.10, bf16[4,1152,128]{2,1,0:T(8,128)(2,1)} %bitcast.9, f32[4,128]{1,0:T(4,128)} %biases_in.1, f32[512,128]{1,0:T(8,128)} %bitcast.11), custom_call_target="tpu_custom_call" | custom-call | tf_op jit(solution)/shard_map/pallas_call | solution.py:464
  56.5 0.7 %copy.12 = f32[1,2,16,16,128]{4,3,2,1,0:T(8,128)} copy(f32[1,2,16,16,128]{4,3,2,1,0:T(8,128)S(1)} %bitcast.8) | data formatting | bytes 524288
  57.2 0.7 %copy.13 = f32[1,2,16,16,128]{4,3,2,1,0:T(8,128)} copy(f32[1,2,16,16,128]{4,3,2,1,0:T(8,128)S(1)} %bitcast.7) | data formatting | bytes 524288
  57.9 0.6 copy.15
  58.5 1.4 %copy.14 = f32[4,3,3,128,128]{4,3,2,1,0:T(8,128)} copy(f32[4,3,3,128,128]{4,3,2,1,0:T(8,128)S(1)} %bitcast.6) | data formatting | bytes 4718592

commit v2 on v1

--- a/solution.py
+++ b/solution.py
@@ -26,8 +26,7 @@
     weights_in,
     biases_in,
     end_grad_in,
-    ends_out,
-    start_out,
+    both_out,
     wg_out,
     bg_out,
     images,
@@ -92,8 +91,7 @@
     def _():
         pl.semaphore_signal(barrier, inc=1, device_id={"dp": z + 1}, device_id_type=MESH)
 
-    for load in loads:
-        load.wait()
+    loads[0].wait()
     centre = slice(4 * channels, 5 * channels)
     total = weights[0, centre, :].astype(jnp.float32)
     for n in range(1, blocks):
@@ -168,6 +166,9 @@
             @pl.when(is_handed(slot))
             def _():
                 hand_copy(slot).start()
+
+    for load in loads[1:]:
+        load.wait()
 
     zero_row = jnp.zeros((count, 1, width, 3 * channels), low)
     window[:, 0:1] = zero_row
@@ -380,7 +381,7 @@
     corrected = starts + chain_finish(0)
     states_all[z] = corrected
     line_start(0)
-    ends_out[...] = trajectory(z, corrected)
+    both_out[0] = trajectory(z, corrected)
 
     chain_start(1, retreat(z, ends_adj) - back)
     if parts > 1:
@@ -393,7 +394,7 @@
     adjoint = ends_adj + chain_finish(1)
     adj_all[z] = adjoint
     line_start(1)
-    start_out[...] = sweep(z, adjoint)
+    both_out[1] = sweep(z, adjoint)
     for i in range(2, parts - 1):
         line_round(0, i + 1)
         other_trajectory(i)
@@ -461,16 +462,15 @@
     share = rows // groups
     dma = pltpu.SemaphoreType.DMA
     vmem = pl.BlockSpec(memory_space=pltpu.VMEM)
-    ends, start, wg, bg = pl.pallas_call(
+    both, wg, bg = pl.pallas_call(
         functools.partial(kernel, dims),
         out_shape=(
-            pltpu.VMEM((rows, channels), f32),
-            pltpu.VMEM((rows, channels), f32),
+            pltpu.VMEM((2, rows, channels), f32),
             pltpu.VMEM((blocks, 9 * channels, channels), f32),
             pltpu.VMEM((blocks, channels), f32),
         ),
         in_specs=[pl.BlockSpec(memory_space=pltpu.HBM)] * 4,
-        out_specs=(vmem,) * 4,
+        out_specs=(vmem,) * 3,
         scratch_shapes=[
             pltpu.VMEM((rows, channels), f32),
             pltpu.VMEM((blocks, 9 * channels, channels), low),
@@ -509,7 +509,7 @@
         end_grad.reshape(rows, channels),
     )
     shape = (1,) + images.shape
-    return (ends.reshape(shape), start.reshape(shape), wg.reshape(weights.shape), bg)
+    return (both[0].reshape(shape), both[1].reshape(shape), wg.reshape(weights.shape), bg)
 
 
 def solution(mesh):

time: 60 us -> 59.5 us (level)
    unnamed x4 -> x2, local copies, waits for them, and re-layouts: 3.39 us -> 1.99 us
    slice x0 -> x1, local copies, waits for them, and re-layouts: none -> 0.82 us  [shards(): both[1].reshape(shape)]
where the time goes in v2:
time: 59.5 us; the launch traced here: 59.3 us
  Pallas kernels  55.9 us (94%)
  local copies, waits for them, and re-layouts  2.81 us (5%)
  between operations  0.64 us (1%)
    pallas_call x1, Pallas kernels, shards(): pl.pallas_call(functools.partial(kernel, dims), out_shape=(pltpu.VMEM((2,...  55.9 us
    unnamed x2, local copies, waits for them, and re-layouts  1.99 us

profile of v2, /device:TPU:0, one launch (start us, length us, event | category | flops | bytes accessed | tf_op | source)
XLA Modules:
  0.0 59.3 jit_solution(13983924762610491863)
XLA Ops:
  0.6 55.9 %shard_map.75 = (f32[2,512,128]{2,1,0:T(8,128)S(1)}, f32[4,1152,128]{2,1,0:T(8,128)S(1)}, f32[4,128]{1,0:T(4,128)S(1)}) custom-call(f32[512,128]{1,0:T(8,128)} %bitcast.8, bf16[4,1152,128]{2,1,0:T(8,128)(2,1)} %bitcast.7, f32[4,128]{1,0:T(4,128)} %biases_in.1, f32[512,128]{1,0:T(8,128)} %bitcast.9), custom_call_target="tpu_custom_call" | custom-call | tf_op jit(solution)/shard_map/pallas_call | solution.py:465
  56.5 1.4 %copy.10 = f32[4,3,3,128,128]{4,3,2,1,0:T(8,128)} copy(f32[4,3,3,128,128]{4,3,2,1,0:T(8,128)S(1)} %bitcast.6) | data formatting | bytes 4718592
  57.9 0.8 %fusion = (f32[1,512,128]{2,1,0:T(8,128)}, f32[1,512,128]{2,1,0:T(8,128)}) fusion(f32[2,512,128]{2,1,0:T(8,128)S(1)} %get-tuple-element.7), kind=kLoop, calls=%fused_computation | loop fusion | bytes 1048576 | tf_op jit(solution)/shard_map/slice | solution.py:512
  58.7 0.6 copy.11
